TPU v7x, 256 devices: a whole 4x4x8 slice. The times are simulated.
256 devices in a mesh: view: 16 (over z, y_hi), tok: 16 (over y_lo, x, core).
Axes of the slice: x: 4, y: 4 (y_hi: 2, y_lo: 2; y = y_hi * 2 + y_lo), z: 8, core: 2. Of those that a mesh axis runs over, the one named last changes fastest.
Arguments:
- q1: bfloat16 [16, 512, 1024], P('view', 'tok'), may hold values from -96 to 96
- k1: bfloat16 [16, 512, 1024], P('view', 'tok'), may hold values from -6 to 6
- v1: bfloat16 [16, 512, 1024], P('view', 'tok'), may hold values from -6 to 6
- nbr: int32 [16, 7], P('view'), may hold values from 0 to 15, as said below
- x2: bfloat16 [16, 512, 1024], P('view', 'tok'), may hold values from -6 to 6
- w_view_out: bfloat16 [1024, 1024], replicated, may hold values from -0.1875 to 0.1875
- norm_gain: float32 [1024], replicated, may hold values from 0.5 to 1.5
- w_qkv: bfloat16 [1024, 3072], replicated, may hold values from -0.1875 to 0.1875
- w_out: bfloat16 [1024, 1024], replicated, may hold values from -0.1875 to 0.1875
Outputs:
- view_feats: float32 [16, 512, 1024], P('view', 'tok')
- lrm_out: float32 [16, 512, 1024], P('view', 'tok')
Inputs may be any that keep to these rules, and one draw needn't show every extreme that they name: `nbr`: row v lists 7 distinct view indices, none equal to v.
All inputs are finite; a program needn't handle non-finite values.
Results may differ from a plain program's by a relative error of at most 0.014.
Values may be sent and summed in bfloat16 or wider, within the bound.
A program may use at most 128 MiB of HBM per device.

v0:
```python
import jax
import jax.numpy as jnp
from jax import lax
from jax.sharding import PartitionSpec as P

H1 = 16
HD1 = 64
HD2 = 64
EPSILON = 1e-06
NEGATIVE = -1e30


def absorb(running, queries, key_piece, val_piece, keep_key, factor_scale):
    running_max, row_total, weighted = running
    scores = (
        jnp.einsum("qhd,khd->qhk", queries, key_piece, preferred_element_type=jnp.float32)
        * factor_scale
    )
    scores = jnp.where(keep_key[None, None, :], scores, NEGATIVE)
    new_max = jnp.maximum(running_max, jnp.max(scores, axis=-1))
    weights = jnp.where(keep_key[None, None, :], jnp.exp(scores - new_max[..., None]), 0.0)
    row_total = jnp.sum(weights, axis=-1)
    weighted = jnp.einsum(
        "qhk,khd->qhd", weights.astype(jnp.bfloat16), val_piece, preferred_element_type=jnp.float32
    )
    return (new_max, row_total, weighted)


def per_device(q1, k1, v1, nbr, x2, w_view_out, norm_gain, w_qkv, w_out):
    own_view = lax.axis_index("view")
    wanted = nbr[0]
    queries = lax.all_gather(q1, "tok", axis=1, tiled=True)[0].reshape(-1, H1, HD1)
    query_rows = queries.shape[0]
    start_state = (
        jnp.full((query_rows, H1), NEGATIVE, jnp.float32),
        jnp.zeros((query_rows, H1), jnp.float32),
        jnp.zeros((query_rows, H1, HD1), jnp.float32),
    )
    scale_one = HD1 ** (-0.5)
    key_piece = lax.all_gather(k1, "view", axis=0, tiled=True)
    val_piece = lax.all_gather(v1, "view", axis=0, tiled=True)
    view_ids = jnp.arange(key_piece.shape[0], dtype=jnp.int32)
    keep_view = (view_ids == own_view) | jnp.any(view_ids[:, None] == wanted[None, :], axis=1)
    keep_key = jnp.repeat(keep_view, key_piece.shape[1])
    running_max, row_total, weighted = absorb(
        start_state,
        queries,
        key_piece.reshape(-1, H1, HD1),
        val_piece.reshape(-1, H1, HD1),
        keep_key,
        scale_one,
    )
    tok_devs = lax.axis_size("tok")
    my_rows = query_rows // tok_devs
    row_peak = lax.pmax(running_max, "tok")
    factor = jnp.exp(running_max - row_peak)
    summed, totals = (
        lax.psum_scatter(weighted * factor[..., None], "tok", scatter_dimension=0, tiled=True),
        lax.psum_scatter(row_total * factor, "tok", scatter_dimension=0, tiled=True),
    )
    attn_one = (summed / totals[..., None]).reshape(my_rows, -1)
    features = attn_one * lax.rsqrt(jnp.mean(attn_one * attn_one, axis=-1, keepdims=True) + EPSILON)
    features_half = features.astype(jnp.bfloat16)
    hidden = x2[0].astype(jnp.float32) + jnp.dot(
        features_half, w_view_out, preferred_element_type=jnp.float32
    )
    normed = (
        hidden * lax.rsqrt(jnp.mean(hidden * hidden, axis=-1, keepdims=True) + EPSILON) * norm_gain
    ).astype(jnp.bfloat16)
    projected = (
        jnp.dot(normed, w_qkv, preferred_element_type=jnp.float32)
        .astype(jnp.bfloat16)
        .reshape(my_rows, 3, -1)
    )
    by_head = lax.all_to_all(projected, "tok", split_axis=2, concat_axis=0, tiled=True)
    local_heads = by_head.shape[2] // HD2
    head_queries = by_head[:, 0].reshape(-1, local_heads, HD2)
    view_rows = head_queries.shape[0]
    scale_two = HD2 ** (-0.5)
    second_state = (
        jnp.full((view_rows, local_heads), NEGATIVE, jnp.float32),
        jnp.zeros((view_rows, local_heads), jnp.float32),
        jnp.zeros((view_rows, local_heads, HD2), jnp.float32),
    )
    key_piece = lax.all_gather(by_head[:, 1], "view", axis=0, tiled=True)
    val_piece = lax.all_gather(by_head[:, 2], "view", axis=0, tiled=True)
    keep_key = jnp.ones((key_piece.shape[0],), jnp.bool_)
    second_max, second_total, second_sum = absorb(
        second_state,
        head_queries,
        key_piece.reshape(-1, local_heads, HD2),
        val_piece.reshape(-1, local_heads, HD2),
        keep_key,
        scale_two,
    )
    attn_two = (second_sum / second_total[..., None]).reshape(view_rows, -1).astype(jnp.bfloat16)
    returned = lax.all_to_all(attn_two, "tok", split_axis=0, concat_axis=1, tiled=True)
    wide = returned.astype(jnp.float32)
    unit_rows = (wide * lax.rsqrt(jnp.mean(wide * wide, axis=-1, keepdims=True) + EPSILON)).astype(
        jnp.bfloat16
    )
    result = jnp.dot(unit_rows, w_out, preferred_element_type=jnp.float32)
    return (features[None], result[None])


def solution(mesh):
    return jax.shard_map(
        per_device,
        mesh=mesh,
        in_specs=(
            P("view", "tok", None),
            P("view", "tok", None),
            P("view", "tok", None),
            P("view", None),
            P("view", "tok", None),
            P(),
            P(),
            P(),
            P(),
        ),
        out_specs=(P("view", "tok", None), P("view", "tok", None)),
        check_vma=False,
    )
```

profile of v0, /device:TPU:1, one launch (start us, length us, event | category | flops | bytes accessed | tf_op | source)
XLA Modules:
  0.0 568.1 jit_solution(11776893962329701940)
XLA Ops:
  7.2 0.0 copy-start
  7.2 0.0 all-gather.8.cloned.1.call-start
  7.2 0.7 all-gather.8.cloned.1.call-update
  7.9 0.0 all-gather.10.cloned.1.call-start
  8.0 0.7 all-gather.10.cloned.1.call-update
  8.7 0.0 all-gather.12.cloned.1.call-start
  8.7 0.7 all-gather.12.cloned.1.call-update
  9.4 0.0 reduce-scatter.7.cloned.1.call-start
  9.4 0.7 fusion.49
  10.2 0.1 broadcast_in_dim.57
  10.3 0.1 broadcast_in_dim.58
  10.4 78.4 %all-gather.8.cloned.1.call-done = bf16[16,32,1024]{2,1,0:T(8,128)(2,1)} async-done(((bf16[1,32,1024]{2,1,0:T(8,128)(2,1)}), bf16[16,32,1024]{2,1,0:T(8,128)(2,1)}) %all-gather.8.cloned.1.call-update) | async-done | bytes 1048592 | tf_op jit(solution)/shard_map/all_gather | solution.py:40
  88.8 4.1 reshape.120
  92.8 33.8 %all-gather.10.cloned.1.call-done = bf16[1,512,1024]{2,1,0:T(8,128)(2,1)} async-done(((bf16[1,32,1024]{2,1,0:T(8,128)(2,1)}), bf16[1,512,1024]{2,1,0:T(8,128)(2,1)}) %all-gather.10.cloned.1.call-update) | async-done | bytes 1048592 | tf_op jit(solution)/shard_map/all_gather | solution.py:32
  126.6 1.5 copy.56
  128.1 9.1 %bitcast_reduce_fusion = (f32[512,16]{0,1:T(8,128)S(1)}, f32[16,512,512]{2,1,0:T(8,128)}) fusion(pred[512]{0:T(512)(128)(4,1)S(1)} %broadcast_in_dim.58, bf16[512,16,64]{0,2,1:T(8,128)(2,1)S(1)} %bitcast.104, bf16[512,16,64]{2,1,0:T(8,128)(2,1)} %reshape.120), kind=kOutput, calls=%fused_computation.3 | convolution fusion | flops 549445632 | bytes 18907648 | tf_op jit(solution)/shard_map/qhd,khd->qhk/dot_general | solution.py:16
  137.2 50.7 %pmax.7 = f32[512,16]{0,1:T(8,128)S(1)} all-reduce(f32[512,16]{0,1:T(8,128)S(1)} %broadcast_maximum_fusion), channel_id=1, replica_groups=mesh['view'=16,'tok'=16] {'tok'}, use_global_device_ids=true, to_apply=%region_2.3 | all-reduce | flops 8192 | bytes 65536 | tf_op jit(solution)/shard_map/pmax | solution.py:55
  187.8 8.2 %fusion.5 = f32[512,16]{0,1:T(8,128)S(1)} fusion(f32[16,512,512]{2,1,0:T(8,128)} %get-tuple-element.9, f32[512,16]{0,1:T(8,128)S(1)} %broadcast_maximum_fusion, pred[512]{0:T(512)(128)(4,1)S(1)} %broadcast_in_dim.58), kind=kLoop, calls=%fused_computation.10 | loop fusion | flops 20963328 | bytes 16843264 | tf_op jit(solution)/shard_map/reduce_sum | solution.py:22
  196.0 0.8 copy.73
  196.9 0.0 reduce-scatter.7.cloned.1.call-update
  196.9 0.0 reduce-scatter.5.cloned.1.call-start
  196.9 6.2 %all-gather.12.cloned.1.call-done = bf16[16,32,1024]{2,1,0:T(8,128)(2,1)} async-done(((bf16[1,32,1024]{2,1,0:T(8,128)(2,1)}), bf16[16,32,1024]{2,1,0:T(8,128)(2,1)}) %all-gather.12.cloned.1.call-update) | async-done | bytes 1048592 | tf_op jit(solution)/shard_map/all_gather | solution.py:41
  203.1 4.1 reshape.121
  207.1 0.0 copy-start.1
  207.1 0.0 copy-start.2
  207.1 11.6 %bitcast_multiply_fusion = f32[512,16,64]{0,2,1:T(8,128)} fusion(f32[16,512,512]{2,1,0:T(8,128)} %get-tuple-element.9, f32[512,16]{0,1:T(8,128)S(1)} %broadcast_maximum_fusion, pred[512]{0:T(512)(128)(4,1)S(1)} %broadcast_in_dim.58, bf16[512,16,64]{2,1,0:T(8,128)(2,1)} %reshape.121, f32[512,16]{0,1:T(8,128)S(1)} %get-tuple-element.5), kind=kOutput, calls=%fused_computation.21 | convolution fusion | flops 558366720 | bytes 19988992 | tf_op jit(solution)/shard_map/qhk,khd->qhd/dot_general | solution.py:23
  218.8 4.8 copy.60
  223.6 0.0 reduce-scatter.5.cloned.1.call-update
  223.6 0.2 all-gather.16.cloned.1.call-start
  223.9 42.9 %reduce-scatter.7.cloned.1.call-done = f32[32,16]{1,0:T(8,128)} async-done(((f32[512,16]{1,0:T(8,128)}), f32[32,16]{1,0:T(8,128)}) %reduce-scatter.7.cloned.1.call-update) | async-done | bytes 2064 | tf_op jit(solution)/shard_map/reduce_scatter | solution.py:59
  266.7 70.7 %reduce-scatter.5.cloned.1.call-done = f32[32,16,64]{2,1,0:T(8,128)} async-done(((f32[512,16,64]{2,1,0:T(8,128)}), f32[32,16,64]{2,1,0:T(8,128)}) %reduce-scatter.5.cloned.1.call-update) | async-done | bytes 131088 | tf_op jit(solution)/shard_map/reduce_scatter | solution.py:58
  337.4 1.5 multiply_reduce_fusion.1
  338.9 0.1 reshape.123
  339.1 0.0 copy-done
  339.1 0.0 copy-done.1
  339.1 0.6 multiply_reduce_fusion.2
  339.7 0.0 copy-done.2
  339.7 4.0 convolution_convert_fusion
  343.7 1.0 reshape.124
  344.7 1.8 copy.62
  346.5 1.4 reshape.133
  347.9 14.7 %all_to_all.28 = bf16[16,2,3072]{2,1,0:T(2,128)(2,1)} all-to-all(bf16[16,2,3072]{2,1,0:T(2,128)(2,1)} %reshape.133), channel_id=1, replica_groups=mesh['view'=16,'tok'=16] {'tok'}, dimensions={0} | all-to-all | bytes 393216 | tf_op jit(solution)/shard_map/all_to_all | solution.py:75
  362.6 1.6 reshape.134
  364.2 1.3 copy.72
  365.4 1.7 fusion.55
  367.1 0.0 all-gather.16.cloned.1.call-update
  367.1 0.0 all-gather.14.cloned.1.call-start
  367.2 0.7 all-gather.14.cloned.1.call-update
  367.9 0.1 reshape.122
  368.0 79.9 %all-gather.16.cloned.1.call-done = bf16[8192,1,64]{2,0,1:T(8,128)(2,1)} async-done(((bf16[512,1,64]{2,0,1:T(8,128)(2,1)}), bf16[8192,1,64]{2,0,1:T(8,128)(2,1)}) %all-gather.16.cloned.1.call-update) | async-done | bytes 1048592 | tf_op jit(solution)/shard_map/all_gather | solution.py:85
  447.9 9.6 %multiply_reduce_fusion = (f32[512]{0:T(512)S(1)}, f32[8192,512]{1,0:T(8,128)}) fusion(bf16[512,3,64]{2,0,1:T(8,128)(2,1)} %bitcast.108, bf16[8192,1,64]{2,0,1:T(8,128)(2,1)} %all-gather.16.cloned.1.call-done), kind=kOutput, calls=%fused_computation.7 | convolution fusion | flops 545259008 | bytes 19007488 | tf_op jit(solution)/shard_map/qhd,khd->qhk/dot_general | solution.py:16
  457.6 8.6 %fusion.3 = f32[512]{0:T(512)S(1)} fusion(f32[8192,512]{1,0:T(8,128)} %get-tuple-element.13, f32[512]{0:T(512)S(1)} %broadcast_maximum_fusion.1), kind=kLoop, calls=%fused_computation.8 | loop fusion | flops 12582400 | bytes 16781312 | tf_op jit(solution)/shard_map/reduce_sum | solution.py:22
  466.2 67.0 %all-gather.14.cloned.1.call-done = bf16[8192,1,64]{2,0,1:T(8,128)(2,1)} async-done(((bf16[512,1,64]{2,0,1:T(8,128)(2,1)}), bf16[8192,1,64]{2,0,1:T(8,128)(2,1)}) %all-gather.14.cloned.1.call-update) | async-done | bytes 1048592 | tf_op jit(solution)/shard_map/all_gather | solution.py:86
  533.2 9.3 %fusion.39 = bf16[512,1,64]{0,2,1:T(8,128)(2,1)S(1)} fusion(f32[8192,512]{1,0:T(8,128)} %get-tuple-element.13, f32[512]{0:T(512)S(1)} %broadcast_maximum_fusion.1, bf16[8192,1,64]{2,0,1:T(8,128)(2,1)} %all-gather.14.cloned.1.call-done, f32[512]{0:T(512)S(1)} %fusion.3), kind=kOutput, calls=%fused_computation.30 | convolution fusion | flops 549519360 | bytes 17895424 | tf_op jit(solution)/shard_map/qhk,khd->qhd/dot_general | solution.py:23
  542.5 0.1 copy.68
  542.7 0.8 reshape.135
  543.4 8.6 %all-to-all-start.1 = ((bf16[16,2,1024]{2,1,0:T(2,128)(2,1)}), bf16[16,2,1024]{2,1,0:T(2,128)(2,1)S(1)}, u32[]{:S(2)}, u32[]{:S(2)}) async-start(bf16[16,2,1024]{2,1,0:T(2,128)(2,1)} %reshape.135), calls=%async_computation.2 | async-start | bytes 131072 | tf_op jit(solution)/shard_map/all_to_all | solution.py:97
  552.0 0.7 broadcast_multiply_fusion
  552.8 5.1 all-to-all-done.1
  557.8 0.1 reshape.136
  558.0 0.1 fusion.44
  558.2 0.2 copy.69
  558.3 0.1 reshape.128
  558.5 2.8 convolution_bitcast_fusion
  (8 shorter events, 0.1 us)
Async XLA Ops:
  7.2 331.9 %copy-start = (bf16[1024,1024]{1,0:T(8,128)(2,1)S(1)}, bf16[1024,1024]{1,0:T(8,128)(2,1)}, u32[]{:S(2)}) copy-start(bf16[1024,1024]{1,0:T(8,128)(2,1)} %param.14) | copy-start | bytes 6291460
  7.2 81.6 %all-gather.8.cloned.1.call-start = ((), (), s32[]{:S(2)}) async-start(), calls=%async_computation.4 | async-start | bytes 1114112 | tf_op jit(solution)/shard_map/all_gather | solution.py:40
  7.9 118.7 %all-gather.10.cloned.1.call-start = ((), (), s32[]{:S(2)}) async-start(), calls=%async_computation.5 | async-start | bytes 1114112 | tf_op jit(solution)/shard_map/all_gather | solution.py:32
  8.7 194.4 %all-gather.12.cloned.1.call-start = ((), (), s32[]{:S(2)}) async-start(), calls=%async_computation.6 | async-start | bytes 1114112 | tf_op jit(solution)/shard_map/all_gather | solution.py:41
  9.4 257.3 %reduce-scatter.7.cloned.1.call-start = ((), (), s32[]{:S(2)}) async-start(), calls=%async_computation.10 | async-start | bytes 278528 | tf_op jit(solution)/shard_map/reduce_scatter | solution.py:59
  196.9 140.5 %reduce-scatter.5.cloned.1.call-start = ((), (), s32[]{:S(2)}) async-start(), calls=%async_computation.7 | async-start | bytes 4456448 | tf_op jit(solution)/shard_map/reduce_scatter | solution.py:58
  207.1 131.9 %copy-start.1 = (bf16[1,32,1024]{2,1,0:T(8,128)(2,1)S(1)}, bf16[1,32,1024]{2,1,0:T(8,128)(2,1)}, u32[]{:S(2)}) copy-start(bf16[1,32,1024]{2,1,0:T(8,128)(2,1)} %param.13) | copy-start | bytes 196612
  207.1 132.6 %copy-start.2 = (f32[1024]{0:T(1024)S(1)}, f32[1024]{0:T(1024)}, u32[]{:S(2)}) copy-start(f32[1024]{0:T(1024)} %param.15) | copy-start | bytes 12292
  223.6 224.3 %all-gather.16.cloned.1.call-start = ((), (), s32[]{:S(2)}) async-start(), calls=%async_computation.9 | async-start | bytes 2228224 | tf_op jit(solution)/shard_map/all_gather | solution.py:85
  367.1 166.1 %all-gather.14.cloned.1.call-start = ((), (), s32[]{:S(2)}) async-start(), calls=%async_computation.8 | async-start | bytes 2228224 | tf_op jit(solution)/shard_map/all_gather | solution.py:86
  543.4 14.4 %all-to-all-start.1 = ((bf16[16,2,1024]{2,1,0:T(2,128)(2,1)}), bf16[16,2,1024]{2,1,0:T(2,128)(2,1)S(1)}, u32[]{:S(2)}, u32[]{:S(2)}) async-start(bf16[16,2,1024]{2,1,0:T(2,128)(2,1)} %reshape.135), calls=%async_computation.2 | async-start | bytes 131072 | tf_op jit(solution)/shard_map/all_to_all | solution.py:97
Sparse Core Ops, SparseCore 0:
  10.6 78.1 all-gather.7
  90.6 35.9 all-gather.9
  129.2 73.8 all-gather.11
  205.4 61.2 reduce-scatter.6
  269.1 68.2 reduce-scatter.4
  367.3 80.6 all-gather.15
  451.1 82.0 all-gather.13
where the time goes:
time: 569 us; the launch traced here: 568 us
  waiting for transfers between devices  387 us (68%)
  blocking collectives  65.4 us (11%)
  matrix products  47.1 us (8%)
  local copies, waits for them, and re-layouts  25.7 us (5%)
  other arithmetic  20 us (4%)
  between operations  14.3 us (3%)
  starting transfers between devices  9.04 us (2%)
    all_gather x1, waiting for transfers between devices, per_device(): key_piece = lax.all_gather(by_head[:, 1], 'view', axis=0, tiled=True)  79.9 us
    all_gather x1, waiting for transfers between devices, per_device(): key_piece = lax.all_gather(k1, 'view', axis=0, tiled=True)  78.4 us
    reduce_scatter x1, waiting for transfers between devices, per_device(): lax.psum_scatter(weighted * factor[..., None], 'tok', scatter_dimension=0...  70.7 us
    all_gather x1, waiting for transfers between devices, per_device(): val_piece = lax.all_gather(by_head[:, 2], 'view', axis=0, tiled=True)  67 us
    pmax x1, blocking collectives, per_device(): row_peak = lax.pmax(running_max, 'tok')  50.7 us
    reduce_scatter x1, waiting for transfers between devices, per_device(): lax.psum_scatter(row_total * factor, 'tok', scatter_dimension=0, tiled=True)  42.9 us
    all_gather x1, waiting for transfers between devices, per_device(): lax.all_gather(q1, 'tok', axis=1, tiled=True)[0].reshape(-1, H1, HD1)  33.8 us
    dot_general x2, matrix products, absorb(): jnp.einsum('qhk,khd->qhd', weights.astype(jnp.bfloat16), val_piece, prefe...  21 us
  transfers between devices with their start and end apart: 8, of which 8 were waited for; matrix products, arithmetic and copies ran while one was open for 11% of the time, Pallas kernels for 0%

commit v1 on v0

--- a/solution.py
+++ b/solution.py
@@ -37,7 +37,8 @@
         jnp.zeros((query_rows, H1, HD1), jnp.float32),
     )
     scale_one = HD1 ** (-0.5)
-    key_piece = lax.all_gather(k1, "view", axis=0, tiled=True)
+    repeated = jnp.stack([k1] * lax.axis_size("view"))
+    key_piece = jnp.concatenate(lax.all_to_all(repeated, "view", 0, 0), axis=0)
     val_piece = lax.all_gather(v1, "view", axis=0, tiled=True)
     view_ids = jnp.arange(key_piece.shape[0], dtype=jnp.int32)
     keep_view = (view_ids == own_view) | jnp.any(view_ids[:, None] == wanted[None, :], axis=1)

time: 569 us -> 498 us (0.88)
  waiting for transfers between devices: 387 us -> 301 us
  starting transfers between devices: 9.04 us -> 20.7 us
    all_gather x1 -> x0, waiting for transfers between devices: 78.4 us -> none  [per_device(): key_piece = lax.all_gather(k1, 'view', axis=0, tiled=True)]
    all_gather x1, waiting for transfers between devices: 33.8 us -> 0.01 us  [per_device(): lax.all_gather(q1, 'tok', axis=1, tiled=True)[0].reshape(-1, H1, HD1)]
    all_to_all x0 -> x1, waiting for transfers between devices: none -> 25.2 us  [per_device(): key_piece = jnp.concatenate(lax.all_to_all(repeated, 'view', 0, 0), axis=0)]
    all_to_all x0 -> x1, starting transfers between devices: none -> 11.7 us  [per_device(): key_piece = jnp.concatenate(lax.all_to_all(repeated, 'view', 0, 0), axis=0)]
  transfers between devices with their start and end apart: 8 -> 8, of which waited for: 8 -> 7; matrix products, arithmetic and copies ran while one was open for 11% -> 13% of each run, Pallas kernels for 0% -> 0%
where the time goes in v1:
time: 498 us; the launch traced here: 497 us
  waiting for transfers between devices  301 us (60%)
  blocking collectives  67.6 us (14%)
  matrix products  47.1 us (9%)
  local copies, waits for them, and re-layouts  26 us (5%)
  starting transfers between devices  20.7 us (4%)
  other arithmetic  20 us (4%)
  between operations  14.3 us (3%)
    all_gather x1, waiting for transfers between devices, per_device(): key_piece = lax.all_gather(by_head[:, 1], 'view', axis=0, tiled=True)  80.1 us
    reduce_scatter x1, waiting for transfers between devices, per_device(): lax.psum_scatter(weighted * factor[..., None], 'tok', scatter_dimension=0...  70.8 us
    all_gather x1, waiting for transfers between devices, per_device(): val_piece = lax.all_gather(by_head[:, 2], 'view', axis=0, tiled=True)  66.9 us
    pmax x1, blocking collectives, per_device(): row_peak = lax.pmax(running_max, 'tok')  52.9 us
    reduce_scatter x1, waiting for transfers between devices, per_device(): lax.psum_scatter(row_total * factor, 'tok', scatter_dimension=0, tiled=True)  42.9 us
    all_to_all x1, waiting for transfers between devices, per_device(): key_piece = jnp.concatenate(lax.all_to_all(repeated, 'view', 0, 0), axis=0)  25.2 us
    dot_general x2, matrix products, absorb(): jnp.einsum('qhk,khd->qhd', weights.astype(jnp.bfloat16), val_piece, prefe...  21 us
    dot_general x2, matrix products, absorb(): jnp.einsum('qhd,khd->qhk', queries, key_piece, preferred_element_type=jnp...  18.7 us
  transfers between devices with their start and end apart: 8, of which 7 were waited for; matrix products, arithmetic and copies ran while one was open for 13% of the time, Pallas kernels for 0%

profile of v1, /device:TPU:1, one launch (start us, length us, event | category | flops | bytes accessed | tf_op | source)
XLA Modules:
  0.0 497.0 jit_solution(14444554555558259861)
XLA Ops:
  7.2 0.0 copy-start
  7.2 0.0 all-gather.7.cloned.1.call-start
  7.2 0.7 all-gather.7.cloned.1.call-update
  7.9 2.0 stack.2
  9.9 11.7 %all-to-all-start = ((bf16[16,1,32,1024]{3,2,1,0:T(8,128)(2,1)}), bf16[16,1,32,1024]{3,2,1,0:T(8,128)(2,1)S(1)}, u32[]{:S(2)}, u32[]{:S(2)}) async-start(bf16[16,1,32,1024]{3,2,1,0:T(8,128)(2,1)} %stack.2), calls=%async_computation | async-start | bytes 2097152 | tf_op jit(solution)/shard_map/all_to_all | solution.py:41
  21.7 0.0 all-gather.9.cloned.1.call-start
  21.7 0.7 all-gather.9.cloned.1.call-update
  22.4 0.0 reduce-scatter.7.cloned.1.call-start
  22.5 0.7 fusion.49
  23.2 0.1 broadcast_in_dim.57
  23.3 0.1 broadcast_in_dim.58
  23.4 25.2 %all-to-all-done = bf16[16,1,32,1024]{3,2,1,0:T(8,128)(2,1)S(1)} async-done(((bf16[16,1,32,1024]{3,2,1,0:T(8,128)(2,1)}), bf16[16,1,32,1024]{3,2,1,0:T(8,128)(2,1)S(1)}, u32[]{:S(2)}, u32[]{:S(2)}) %all-to-all-start) | async-done | bytes 1048608 | tf_op jit(solution)/shard_map/all_to_all | solution.py:41
  48.6 2.4 reshape_reshape.3
  50.9 0.0 all-gather.7.cloned.1.call-done
  50.9 1.5 copy.56
  52.4 9.1 %bitcast_reduce_fusion = (f32[512,16]{0,1:T(8,128)S(1)}, f32[16,512,512]{2,1,0:T(8,128)}) fusion(pred[512]{0:T(512)(128)(4,1)S(1)} %broadcast_in_dim.58, bf16[512,16,64]{0,2,1:T(8,128)(2,1)S(1)} %bitcast.107, bf16[512,16,64]{2,1,0:T(8,128)(2,1)} %reshape_reshape.3), kind=kOutput, calls=%fused_computation.3 | convolution fusion | flops 549445632 | bytes 18907648 | tf_op jit(solution)/shard_map/qhd,khd->qhk/dot_general | solution.py:16
  61.5 52.9 %pmax.7 = f32[512,16]{0,1:T(8,128)S(1)} all-reduce(f32[512,16]{0,1:T(8,128)S(1)} %broadcast_maximum_fusion), channel_id=1, replica_groups=mesh['view'=16,'tok'=16] {'tok'}, use_global_device_ids=true, to_apply=%region_2.3 | all-reduce | flops 8192 | bytes 65536 | tf_op jit(solution)/shard_map/pmax | solution.py:56
  114.4 8.1 %fusion.5 = f32[512,16]{0,1:T(8,128)S(1)} fusion(f32[16,512,512]{2,1,0:T(8,128)} %get-tuple-element.9, f32[512,16]{0,1:T(8,128)S(1)} %broadcast_maximum_fusion, pred[512]{0:T(512)(128)(4,1)S(1)} %broadcast_in_dim.58), kind=kLoop, calls=%fused_computation.10 | loop fusion | flops 20963328 | bytes 16843264 | tf_op jit(solution)/shard_map/reduce_sum | solution.py:22
  122.6 0.8 copy.73
  123.4 0.0 reduce-scatter.7.cloned.1.call-update
  123.5 0.0 reduce-scatter.5.cloned.1.call-start
  123.5 8.5 %all-gather.9.cloned.1.call-done = bf16[16,32,1024]{2,1,0:T(8,128)(2,1)} async-done(((bf16[1,32,1024]{2,1,0:T(8,128)(2,1)}), bf16[16,32,1024]{2,1,0:T(8,128)(2,1)}) %all-gather.9.cloned.1.call-update) | async-done | bytes 1048592 | tf_op jit(solution)/shard_map/all_gather | solution.py:42
  132.0 4.1 reshape.120
  136.1 0.0 copy-start.1
  136.1 0.0 copy-start.2
  136.1 11.6 %bitcast_multiply_fusion = f32[512,16,64]{0,2,1:T(8,128)} fusion(f32[16,512,512]{2,1,0:T(8,128)} %get-tuple-element.9, f32[512,16]{0,1:T(8,128)S(1)} %broadcast_maximum_fusion, pred[512]{0:T(512)(128)(4,1)S(1)} %broadcast_in_dim.58, bf16[512,16,64]{2,1,0:T(8,128)(2,1)} %reshape.120, f32[512,16]{0,1:T(8,128)S(1)} %get-tuple-element.5), kind=kOutput, calls=%fused_computation.21 | convolution fusion | flops 558366720 | bytes 19988992 | tf_op jit(solution)/shard_map/qhk,khd->qhd/dot_general | solution.py:23
  147.7 4.8 copy.60
  152.6 0.0 reduce-scatter.5.cloned.1.call-update
  152.6 0.2 all-gather.13.cloned.1.call-start
  152.8 42.9 %reduce-scatter.7.cloned.1.call-done = f32[32,16]{1,0:T(8,128)} async-done(((f32[512,16]{1,0:T(8,128)}), f32[32,16]{1,0:T(8,128)}) %reduce-scatter.7.cloned.1.call-update) | async-done | bytes 2064 | tf_op jit(solution)/shard_map/reduce_scatter | solution.py:60
  195.7 70.8 %reduce-scatter.5.cloned.1.call-done = f32[32,16,64]{2,1,0:T(8,128)} async-done(((f32[512,16,64]{2,1,0:T(8,128)}), f32[32,16,64]{2,1,0:T(8,128)}) %reduce-scatter.5.cloned.1.call-update) | async-done | bytes 131088 | tf_op jit(solution)/shard_map/reduce_scatter | solution.py:59
  266.5 1.5 multiply_reduce_fusion.1
  268.0 0.1 reshape.122
  268.2 0.0 copy-done
  268.2 0.0 copy-done.1
  268.2 0.6 multiply_reduce_fusion.2
  268.8 0.0 copy-done.2
  268.8 4.0 convolution_convert_fusion
  272.8 1.0 reshape.123
  273.8 1.8 copy.62
  275.6 1.4 reshape.132
  277.0 14.7 %all_to_all.33 = bf16[16,2,3072]{2,1,0:T(2,128)(2,1)} all-to-all(bf16[16,2,3072]{2,1,0:T(2,128)(2,1)} %reshape.132), channel_id=1, replica_groups=mesh['view'=16,'tok'=16] {'tok'}, dimensions={0} | all-to-all | bytes 393216 | tf_op jit(solution)/shard_map/all_to_all | solution.py:76
  291.7 1.6 reshape.133
  293.3 1.3 copy.72
  294.5 1.7 fusion.55
  296.2 0.0 all-gather.13.cloned.1.call-update
  296.3 0.0 all-gather.11.cloned.1.call-start
  296.3 0.5 all-gather.11.cloned.1.call-update
  296.8 0.1 reshape.121
  297.0 80.1 %all-gather.13.cloned.1.call-done = bf16[8192,1,64]{2,0,1:T(8,128)(2,1)} async-done(((bf16[512,1,64]{2,0,1:T(8,128)(2,1)}), bf16[8192,1,64]{2,0,1:T(8,128)(2,1)}) %all-gather.13.cloned.1.call-update) | async-done | bytes 1048592 | tf_op jit(solution)/shard_map/all_gather | solution.py:86
  377.1 9.6 %multiply_reduce_fusion = (f32[512]{0:T(512)S(1)}, f32[8192,512]{1,0:T(8,128)}) fusion(bf16[512,3,64]{2,0,1:T(8,128)(2,1)} %bitcast.111, bf16[8192,1,64]{2,0,1:T(8,128)(2,1)} %all-gather.13.cloned.1.call-done), kind=kOutput, calls=%fused_computation.7 | convolution fusion | flops 545259008 | bytes 19007488 | tf_op jit(solution)/shard_map/qhd,khd->qhk/dot_general | solution.py:16
  386.7 8.6 %fusion.3 = f32[512]{0:T(512)S(1)} fusion(f32[8192,512]{1,0:T(8,128)} %get-tuple-element.13, f32[512]{0:T(512)S(1)} %broadcast_maximum_fusion.1), kind=kLoop, calls=%fused_computation.8 | loop fusion | flops 12582400 | bytes 16781312 | tf_op jit(solution)/shard_map/reduce_sum | solution.py:22
  395.3 66.9 %all-gather.11.cloned.1.call-done = bf16[8192,1,64]{2,0,1:T(8,128)(2,1)} async-done(((bf16[512,1,64]{2,0,1:T(8,128)(2,1)}), bf16[8192,1,64]{2,0,1:T(8,128)(2,1)}) %all-gather.11.cloned.1.call-update) | async-done | bytes 1048592 | tf_op jit(solution)/shard_map/all_gather | solution.py:87
  462.2 9.3 %fusion.39 = bf16[512,1,64]{0,2,1:T(8,128)(2,1)S(1)} fusion(f32[8192,512]{1,0:T(8,128)} %get-tuple-element.13, f32[512]{0:T(512)S(1)} %broadcast_maximum_fusion.1, bf16[8192,1,64]{2,0,1:T(8,128)(2,1)} %all-gather.11.cloned.1.call-done, f32[512]{0:T(512)S(1)} %fusion.3), kind=kOutput, calls=%fused_computation.30 | convolution fusion | flops 549519360 | bytes 17895424 | tf_op jit(solution)/shard_map/qhk,khd->qhd/dot_general | solution.py:23
  471.5 0.1 copy.68
  471.6 0.8 reshape.134
  472.4 8.6 %all-to-all-start.2 = ((bf16[16,2,1024]{2,1,0:T(2,128)(2,1)}), bf16[16,2,1024]{2,1,0:T(2,128)(2,1)S(1)}, u32[]{:S(2)}, u32[]{:S(2)}) async-start(bf16[16,2,1024]{2,1,0:T(2,128)(2,1)} %reshape.134), calls=%async_computation.3 | async-start | bytes 131072 | tf_op jit(solution)/shard_map/all_to_all | solution.py:98
  481.0 0.7 broadcast_multiply_fusion
  481.7 5.1 %all-to-all-done.2 = bf16[16,2,1024]{2,1,0:T(2,128)(2,1)S(1)} async-done(((bf16[16,2,1024]{2,1,0:T(2,128)(2,1)}), bf16[16,2,1024]{2,1,0:T(2,128)(2,1)S(1)}, u32[]{:S(2)}, u32[]{:S(2)}) %all-to-all-start.2) | async-done | bytes 65568 | tf_op jit(solution)/shard_map/all_to_all | solution.py:98
  486.8 0.1 reshape.135
  487.0 0.1 fusion.44
  487.1 0.2 copy.69
  487.3 0.1 reshape.127
  487.4 2.8 convolution_bitcast_fusion
  (8 shorter events, 0.1 us)
Async XLA Ops:
  7.2 261.0 %copy-start = (bf16[1024,1024]{1,0:T(8,128)(2,1)S(1)}, bf16[1024,1024]{1,0:T(8,128)(2,1)}, u32[]{:S(2)}) copy-start(bf16[1024,1024]{1,0:T(8,128)(2,1)} %param.14) | copy-start | bytes 6291460
  7.2 43.8 %all-gather.7.cloned.1.call-start = ((), (), s32[]{:S(2)}) async-start(), calls=%async_computation.5 | async-start | bytes 1114112 | tf_op jit(solution)/shard_map/all_gather | solution.py:32
  9.9 38.7 %all-to-all-start = ((bf16[16,1,32,1024]{3,2,1,0:T(8,128)(2,1)}), bf16[16,1,32,1024]{3,2,1,0:T(8,128)(2,1)S(1)}, u32[]{:S(2)}, u32[]{:S(2)}) async-start(bf16[16,1,32,1024]{3,2,1,0:T(8,128)(2,1)} %stack.2), calls=%async_computation | async-start | bytes 2097152 | tf_op jit(solution)/shard_map/all_to_all | solution.py:41
  21.7 110.4 %all-gather.9.cloned.1.call-start = ((), (), s32[]{:S(2)}) async-start(), calls=%async_computation.6 | async-start | bytes 1114112 | tf_op jit(solution)/shard_map/all_gather | solution.py:42
  22.4 173.3 %reduce-scatter.7.cloned.1.call-start = ((), (), s32[]{:S(2)}) async-start(), calls=%async_computation.10 | async-start | bytes 278528 | tf_op jit(solution)/shard_map/reduce_scatter | solution.py:60
  123.5 143.0 %reduce-scatter.5.cloned.1.call-start = ((), (), s32[]{:S(2)}) async-start(), calls=%async_computation.7 | async-start | bytes 4456448 | tf_op jit(solution)/shard_map/reduce_scatter | solution.py:59
  136.1 132.1 %copy-start.1 = (bf16[1,32,1024]{2,1,0:T(8,128)(2,1)S(1)}, bf16[1,32,1024]{2,1,0:T(8,128)(2,1)}, u32[]{:S(2)}) copy-start(bf16[1,32,1024]{2,1,0:T(8,128)(2,1)} %param.13) | copy-start | bytes 196612
  136.1 132.7 %copy-start.2 = (f32[1024]{0:T(1024)S(1)}, f32[1024]{0:T(1024)}, u32[]{:S(2)}) copy-start(f32[1024]{0:T(1024)} %param.15) | copy-start | bytes 12292
  152.6 224.5 %all-gather.13.cloned.1.call-start = ((), (), s32[]{:S(2)}) async-start(), calls=%async_computation.9 | async-start | bytes 2228224 | tf_op jit(solution)/shard_map/all_gather | solution.py:86
  296.3 165.9 %all-gather.11.cloned.1.call-start = ((), (), s32[]{:S(2)}) async-start(), calls=%async_computation.8 | async-start | bytes 2228224 | tf_op jit(solution)/shard_map/all_gather | solution.py:87
  472.4 14.4 %all-to-all-start.2 = ((bf16[16,2,1024]{2,1,0:T(2,128)(2,1)}), bf16[16,2,1024]{2,1,0:T(2,128)(2,1)S(1)}, u32[]{:S(2)}, u32[]{:S(2)}) async-start(bf16[16,2,1024]{2,1,0:T(2,128)(2,1)} %reshape.134), calls=%async_computation.3 | async-start | bytes 131072 | tf_op jit(solution)/shard_map/all_to_all | solution.py:98
Sparse Core Ops, SparseCore 0:
  9.8 40.9 all-gather.6
  53.4 78.5 all-gather.8
  134.5 61.1 reduce-scatter.6
  198.1 68.3 reduce-scatter.4
  296.4 80.6 all-gather.12
  380.1 82.0 all-gather.10
